TPU v7x, 32 devices: a whole 2x2x4 slice. The times are simulated.
32 devices in a mesh: blocks: 8 (over z, core), lev: 4 (over y, x).
Axes of the slice: x: 2, y: 2, z: 4, core: 2. Of those that a mesh axis runs over, the one named last changes fastest.
Arguments:
- tracers: float32 [8, 4, 8, 128, 128], P('blocks', 'lev'), may hold values from -6 to 6
- east_velocity: float32 [8, 8, 128, 128], P('blocks'), may hold values from -0.24 to 0.24
- north_velocity: float32 [8, 8, 128, 128], P('blocks'), may hold values from -0.24 to 0.24
- upward_velocity: float32 [8, 8, 128, 128], P('blocks'), may hold values from -0.24 to 0.24
- target: float32 [8, 4, 8, 128, 128], P('blocks', 'lev'), may hold values from 0.09375 to 12.65625
- bottom: int32 [8, 128, 128], P('blocks'), may hold values from 0 to 8, as said below
- shave_fraction: float32 [8, 128, 128], P('blocks'), may hold values from 0.05 to 1, as said below
- side_bottom: int32 [8, 4, 128], P('blocks'), may hold values from 0 to 8, as said below
- neighbors: int32 [8, 4], P('blocks'), may hold values from -1 to 7, as said below
- fold_partner: int32 [8], P('blocks'), may hold values from -1 to 7, as said below
- thin_pairs: int32 [8, 2, 128], P('blocks'), may hold values from 0 to 16383, as said below
Outputs:
- new_tracers: float32 [8, 4, 8, 128, 128], P('blocks', 'lev')
Inputs may be any that keep to these rules, and one draw needn't show every extreme that they name: The blocks form a grid of 3 block columns, periodic from west to east, and 4 block rows; entries are mutual: neighbors[b,0] = c exactly when neighbors[c,1] = b, and neighbors[b,2] = c exactly when neighbors[c,3] = b; a block's entries that are not -1 differ; blocks of the top row have -1 to the north. `fold_partner`: set exactly for the blocks of the top row; mutual, a block may be its own partner. `bottom`: every block has wet columns. `side_bottom`: equals the bottom of the adjacent column or row of the neighbouring block, across the north fold the partner's top row in reversed order, 0 where no block lies. `thin_pairs`: thin cells of a block are distinct and have bottom 1 or more; each partner is the cell just east of its thin cell in the same row, with a bottom no smaller; no cell appears twice in a block. `shave_fraction`: listed thin cells have 0.05 to 0.2, all other cells 0.5 to 1.
All inputs are finite; a program needn't handle non-finite values.
Results may differ from a plain program's by a relative error of at most 0.0003.
Values sent between devices are 32-bit elements; how exact they have to be, the bound alone decides.
A program may use at most 64 MiB of HBM per device.

v0:
```python
import functools

import jax
import jax.numpy as jnp
from jax import lax
from jax.experimental import pallas as pl
from jax.experimental.pallas import tpu as pltpu
from jax.sharding import PartitionSpec as P

RATE = 0.5
THIN_LIMIT = 0.35
MESH = pl.DeviceIdType.MESH
F32 = jnp.float32
HIGHEST = lax.Precision.HIGHEST


def upwind(face, first, second):
    return jnp.maximum(face, 0.0) * first + jnp.minimum(face, 0.0) * second


def kernel(
    nb,
    nl,
    nbr_hbm,
    fold_hbm,
    side_hbm,
    t_hbm,
    u_hbm,
    v_hbm,
    w_hbm,
    g_hbm,
    bottom_hbm,
    shave_hbm,
    out_ref,
    tg_ref,
    flow_ref,
    bottom_ref,
    shave_ref,
    nbr_ref,
    fold_ref,
    side_ref,
    x_ref,
    edge_ref,
    pick_ref,
    gain_ref,
    pay_ref,
    halo_ref,
    part_ref,
    parts_ref,
    in_sem,
    edge_send,
    edge_recv,
    part_send,
    part_recv,
):
    t_ref, g_ref = tg_ref.at[0], tg_ref.at[1]
    u_ref, v_ref, w_ref = (flow_ref.at[i] for i in range(3))
    levels, rows, cols = t_ref.shape
    n = nb * nl
    unroll = n <= 64
    block = lax.axis_index("blocks")
    lev = lax.axis_index("lev")
    late = (block >= nb // 2) & (lev > 0)

    def each_other(visit):
        def outer(i, carry):
            there = lax.rem(block + i, nb)

            def inner(j, carry):
                visit(i * nl + j - 1, {"blocks": there, "lev": lax.rem(lev + j, nl)})
                return carry

            return lax.fori_loop(0, nl, inner, carry, unroll=unroll)

        def first(j, carry):
            visit(j - 1, {"blocks": block, "lev": lax.rem(lev + j, nl)})
            return carry

        lax.fori_loop(1, nb, outer, 0, unroll=unroll)
        lax.fori_loop(1, nl, first, 0, unroll=unroll)

    plan = (
        (t_hbm, t_ref, 0),
        (bottom_hbm, bottom_ref, 1),
        (shave_hbm, shave_ref, 2),
        (g_hbm, g_ref, 0),
        (nbr_hbm, nbr_ref, 3),
        (fold_hbm, fold_ref, 4),
        (side_hbm, side_ref, 5),
        (u_hbm, u_ref, 6),
        (v_hbm, v_ref, 6),
        (w_hbm, w_ref, 6),
    )
    for src, dst, sem in plan:
        pltpu.make_async_copy(src, dst, in_sem.at[sem]).start()

    def arrived(ref, sem):
        pltpu.make_async_copy(ref, ref, in_sem.at[sem]).wait()

    barrier = pltpu.get_barrier_semaphore()

    each_other(
        lambda slot, device: pl.semaphore_signal(
            barrier, inc=1, device_id=device, device_id_type=MESH
        )
    )

    lane = lax.broadcasted_iota(jnp.int32, (rows, cols), 1)
    row = lax.broadcasted_iota(jnp.int32, (rows, cols), 0)
    lane_pair = lane // 2

    arrived(bottom_ref, 1)
    arrived(shave_ref, 2)
    arrived(tg_ref, 0)
    bottom = bottom_ref[...]
    shave = shave_ref[...]
    last = bottom - 1
    source = jnp.zeros((rows, cols), F32)
    for k in range(levels):
        thick = jnp.where(k < last, 1.0, jnp.where(k == last, shave, 0.0))
        source += thick * (RATE * (g_ref[k] - t_ref[k]))
    volume = jnp.where(bottom > 0, last.astype(F32) + shave, 0.0)
    source = jnp.sum(source, axis=0, keepdims=True)
    volume = jnp.sum(volume, axis=0, keepdims=True)
    half = cols // 2
    first_half = lax.broadcasted_iota(jnp.int32, (1, cols), 1) < half
    own_part = jnp.where(
        first_half,
        source + pltpu.roll(source, half, 1),
        volume + pltpu.roll(volume, half, 1),
    )
    part_ref[...] = own_part

    def send_parts():
        each_other(
            lambda slot, device: pltpu.make_async_remote_copy(
                src_ref=part_ref,
                dst_ref=parts_ref.at[slot],
                send_sem=part_send,
                recv_sem=part_recv,
                device_id=device,
                device_id_type=MESH,
            ).start()
        )

    @pl.when(late)
    def _():
        pl.semaphore_wait(barrier, n - 1)
        send_parts()

    def strip(fields):
        wide = jnp.zeros((rows, cols), F32)
        for j, field in enumerate(fields):
            wide = jnp.where(lane_pair == j, pltpu.roll(field(), 2 * j + 1, 1), wide)
        return wide.T

    arrived(flow_ref, 6)
    fields = [functools.partial(lambda k: t_ref[k], k) for k in range(levels)]
    fields += [functools.partial(lambda k: u_ref[k], k) for k in range(levels)]
    edge_ref[...] = strip(fields)
    t_east = edge_ref[pl.ds(0, levels, stride=2), :]
    t_west = edge_ref[pl.ds(1, levels, stride=2), :]
    u_east = edge_ref[pl.ds(2 * levels, levels, stride=2), :]
    u_west = edge_ref[pl.ds(2 * levels + 1, levels, stride=2), :]
    t_south = t_ref[:, 0, :]
    t_north = t_ref[:, rows - 1, :]
    v_south = v_ref[:, 0, :]
    v_north = v_ref[:, rows - 1, :]
    mirror = (
        lax.broadcasted_iota(jnp.int32, (cols, cols), 0)
        + lax.broadcasted_iota(jnp.int32, (cols, cols), 1)
        == cols - 1
    ).astype(F32)
    turned = jnp.dot(
        jnp.concatenate([t_north, v_north], 0), mirror, precision=HIGHEST, preferred_element_type=F32
    )
    t_edges = (t_west, t_east, t_south, t_north)
    f_edges = (u_west, u_east, v_south, v_north)
    arrived(nbr_ref, 3)
    arrived(fold_ref, 4)
    arrived(side_ref, 5)
    sides = [nbr_ref[0, s] for s in range(4)]
    fold = fold_ref[0, 0]
    blank = jnp.zeros((levels, cols), F32)

    def pack(i, carry):
        there = lax.rem(block + i, nb)
        t_side, f_side = blank, blank
        for s in range(4):
            hit = sides[s] == there
            t_side = jnp.where(hit, t_edges[s], t_side)
            f_side = jnp.where(hit, f_edges[s], f_side)
        pay_ref[i - 1, :levels, :] = t_side
        pay_ref[i - 1, levels : 2 * levels, :] = f_side
        pay_ref[i - 1, 2 * levels :, :] = turned
        return carry

    lax.fori_loop(1, nb, pack, 0, unroll=unroll)

    @pl.when(jnp.logical_not(late))
    def _():
        pl.semaphore_wait(barrier, n - 1)

    def send_edges(i, carry):
        pltpu.make_async_remote_copy(
            src_ref=pay_ref.at[i - 1],
            dst_ref=halo_ref.at[i - 1],
            send_sem=edge_send,
            recv_sem=edge_recv,
            device_id={"blocks": lax.rem(block + i, nb), "lev": lev},
            device_id_type=MESH,
        ).start()
        return carry

    lax.fori_loop(1, nb, send_edges, 0, unroll=unroll)

    @pl.when(jnp.logical_not(late))
    def _():
        send_parts()

    inverse = 1.0 / shave
    bottom_east = pltpu.roll(bottom, cols - 1, 1)
    open_east = jnp.where(lane == cols - 1, 0, jnp.minimum(bottom, bottom_east))
    open_north = jnp.where(row == rows - 1, 0, jnp.minimum(bottom, pltpu.roll(bottom, rows - 1, 0)))
    partner_shave = jnp.where(bottom_east == bottom, pltpu.roll(shave, cols - 1, 1), 1.0)
    scale = 1.0 / (shave + partner_shave)
    weight = shave * scale
    partner_weight = partner_shave * scale
    struck = jnp.where(shave < THIN_LIMIT, last, -1)
    struck_west = pltpu.roll(struck, 1, 1)

    edge_ref[...] = strip(
        (
            lambda: bottom.astype(F32),
            lambda: shave,
            lambda: jnp.where(lane == 0, weight, pltpu.roll(partner_weight, 1, 1)),
            lambda: jnp.where(lane == 0, struck, struck_west).astype(F32),
        )
    )

    upper = jnp.zeros((rows, cols), F32)
    for k in range(levels):
        t = t_ref[k]
        u = u_ref[k]
        v = v_ref[k]
        face = jnp.where(k < open_east, 0.5 * (u + pltpu.roll(u, cols - 1, 1)), 0.0)
        flux = upwind(face, t, pltpu.roll(t, cols - 1, 1))
        divergence = pltpu.roll(flux, 1, 1) - flux
        face = jnp.where(k < open_north, 0.5 * (v + pltpu.roll(v, rows - 1, 0)), 0.0)
        flux = upwind(face, t, pltpu.roll(t, rows - 1, 0))
        divergence += pltpu.roll(flux, 1, 0) - flux
        if k < levels - 1:
            face = jnp.where(k + 1 < bottom, 0.5 * (w_ref[k] + w_ref[k + 1]), 0.0)
            lower = upwind(face, t_ref[k + 1], t)
        else:
            lower = jnp.zeros((rows, cols), F32)
        divergence += lower - upper
        upper = lower
        x = t + divergence * jnp.where(k == last, inverse, 1.0) + RATE * (g_ref[k] - t)
        merged = weight * x + partner_weight * pltpu.roll(x, cols - 1, 1)
        x = jnp.where(struck == k, merged, x)
        x_ref[k] = jnp.where(struck_west == k, pltpu.roll(merged, 1, 1), x)

    places = (0, 1, cols - 2, cols - 1)
    kinds = len(places)
    source_row = lax.broadcasted_iota(jnp.int32, (kinds * levels, levels * cols), 0)
    target = lax.broadcasted_iota(jnp.int32, (kinds * levels, levels * cols), 1)
    chosen = jnp.zeros((kinds * levels, levels * cols), F32)
    for p, place in enumerate(places):
        chosen = jnp.where(target == (source_row - p * levels) * cols + place, 1.0, chosen)
    chosen = chosen.astype(jnp.bfloat16)
    for p in range(3):
        pick_ref[p * kinds * levels : (p + 1) * kinds * levels, :] = chosen

    grid = lax.broadcasted_iota(jnp.int32, (levels, cols), 0)
    grid_f = grid.astype(F32)
    edge_bottom = (
        edge_ref[1:2, :],
        edge_ref[0:1, :],
        bottom_ref[0:1, :].astype(F32),
        bottom_ref[rows - 1 : rows, :].astype(F32),
    )
    edge_shave = (
        edge_ref[3:4, :],
        edge_ref[2:3, :],
        shave_ref[0:1, :],
        shave_ref[rows - 1 : rows, :],
    )
    wets, scales = [], []
    for s in range(4):
        beyond = side_ref[s : s + 1, :].astype(F32)
        wets.append(grid_f < jnp.minimum(edge_bottom[s], beyond))
        scales.append(jnp.where(grid_f == edge_bottom[s] - 1.0, 1.0 / edge_shave[s], 1.0))
    side_weight = (edge_ref[5:6, :], edge_ref[4:5, :])
    side_struck = (edge_ref[7:8, :] == grid_f, edge_ref[6:7, :] == grid_f)

    found_t = [jnp.where(sides[s] == block, t_edges[s ^ 1], blank) for s in range(4)]
    found_f = [jnp.where(sides[s] == block, f_edges[s ^ 1], blank) for s in range(4)]
    hit = fold == block
    found_t[3] = jnp.where(hit, turned[:levels], found_t[3])
    found_f[3] = jnp.where(hit, -turned[levels:], found_f[3])

    pltpu.make_async_copy(halo_ref, halo_ref, edge_recv).wait()

    def collect(i, carry):
        found_t, found_f = list(carry[0]), list(carry[1])
        origin = lax.rem(block + nb - i, nb)
        side_t, side_f, over_t, over_f = (
            halo_ref[i - 1, p * levels : (p + 1) * levels, :] for p in range(4)
        )
        found_t = [jnp.where(sides[s] == origin, side_t, found_t[s]) for s in range(4)]
        found_f = [jnp.where(sides[s] == origin, side_f, found_f[s]) for s in range(4)]
        hit = fold == origin
        found_t[3] = jnp.where(hit, over_t, found_t[3])
        found_f[3] = jnp.where(hit, -over_f, found_f[3])
        return found_t, found_f

    found_t, found_f = lax.fori_loop(1, nb, collect, (found_t, found_f), unroll=unroll)

    gains = []
    for s in range(4):
        face = jnp.where(wets[s], 0.5 * (f_edges[s] + found_f[s]), 0.0)
        if s % 2 == 0:
            flux = upwind(face, found_t[s], t_edges[s])
        else:
            flux = -upwind(face, t_edges[s], found_t[s])
        gains.append(flux * scales[s])
    west = jnp.where(side_struck[0], side_weight[0] * gains[0], gains[0])
    east = jnp.where(side_struck[1], side_weight[1] * gains[1], gains[1])
    wide = jnp.concatenate(
        [
            west,
            jnp.where(side_struck[0], west, 0.0),
            jnp.where(side_struck[1], east, 0.0),
            east,
        ],
        0,
    )
    high = wide.astype(jnp.bfloat16)
    rest = wide - high.astype(F32)
    middle = rest.astype(jnp.bfloat16)
    low = (rest - middle.astype(F32)).astype(jnp.bfloat16)
    gain_ref[...] = lax.dot_general(
        jnp.concatenate([high, middle, low], 0),
        pick_ref[...],
        (((0,), (0,)), ((), ())),
        preferred_element_type=F32,
    )
    for s, r in ((2, 0), (3, rows - 1)):
        merged = weight[r : r + 1] * gains[s] + partner_weight[r : r + 1] * pltpu.roll(
            gains[s], cols - 1, 1
        )
        gain = jnp.where(struck[r : r + 1] == grid, merged, gains[s])
        gain = jnp.where(struck_west[r : r + 1] == grid, pltpu.roll(merged, 1, 1), gain)
        x_ref[:, r, :] += gain

    pltpu.make_async_copy(parts_ref, parts_ref, part_recv).wait()
    total = lax.fori_loop(
        0, n - 1, lambda i, carry: carry + parts_ref[i], part_ref[...], unroll=unroll
    )
    total_source = jnp.sum(jnp.where(first_half, total, 0.0), axis=1, keepdims=True)
    total_volume = jnp.sum(jnp.where(first_half, 0.0, total), axis=1, keepdims=True)
    mean = total_source / total_volume

    for k in range(levels):
        moved = x_ref[k] + gain_ref[:, k * cols : (k + 1) * cols]
        out_ref[k] = jnp.where(k < bottom_ref[...], moved - mean, 0.0)

    pltpu.make_async_copy(halo_ref, halo_ref, edge_send).wait()
    pltpu.make_async_copy(parts_ref, parts_ref, part_send).wait()


def local(
    nb,
    nl,
    tracers,
    east_velocity,
    north_velocity,
    upward_velocity,
    target,
    bottom,
    shave_fraction,
    side_bottom,
    neighbors,
    fold_partner,
    thin_pairs,
):
    levels, rows, cols = tracers.shape[2:]
    in_hbm = functools.partial(pltpu.with_memory_space_constraint, memory_space=pltpu.HBM)
    cube = (levels, rows, cols)
    n = nb * nl
    vmem = pl.BlockSpec(memory_space=pltpu.VMEM)
    grant = (14 << 20) + 4 * cols * (8 * levels * nb + 8 * n)
    anywhere = pl.BlockSpec(memory_space=pl.ANY)
    stepped = pl.pallas_call(
        functools.partial(kernel, nb, nl),
        out_shape=pltpu.VMEM(cube, F32),
        in_specs=[anywhere] * 10,
        out_specs=vmem,
        scratch_shapes=[
            pltpu.VMEM((2, *cube), F32),
            pltpu.VMEM((3, *cube), F32),
            pltpu.VMEM((rows, cols), jnp.int32),
            pltpu.VMEM((rows, cols), F32),
            pltpu.SMEM((1, 4), jnp.int32),
            pltpu.SMEM((1, 1), jnp.int32),
            pltpu.VMEM((4, cols), jnp.int32),
            pltpu.VMEM(cube, F32),
            pltpu.VMEM((cols, rows), F32),
            pltpu.VMEM((12 * levels, levels * cols), jnp.bfloat16),
            pltpu.VMEM((rows, levels * cols), F32),
            pltpu.VMEM((nb - 1, 4 * levels, cols), F32),
            pltpu.VMEM((nb - 1, 4 * levels, cols), F32),
            pltpu.VMEM((1, cols), F32),
            pltpu.VMEM((n - 1, 1, cols), F32),
            pltpu.SemaphoreType.DMA((7,)),
            pltpu.SemaphoreType.DMA,
            pltpu.SemaphoreType.DMA,
            pltpu.SemaphoreType.DMA,
            pltpu.SemaphoreType.DMA,
        ],
        compiler_params=pltpu.CompilerParams(
            collective_id=0, has_side_effects=True, vmem_limit_bytes=grant
        ),
    )(
        in_hbm(neighbors),
        fold_partner.reshape(1, 1),
        in_hbm(side_bottom.reshape(4, cols)),
        in_hbm(tracers.reshape(cube)),
        in_hbm(east_velocity.reshape(cube)),
        in_hbm(north_velocity.reshape(cube)),
        in_hbm(upward_velocity.reshape(cube)),
        in_hbm(target.reshape(cube)),
        in_hbm(bottom.reshape(rows, cols)),
        in_hbm(shave_fraction.reshape(rows, cols)),
    )
    return stepped.reshape(tracers.shape)


def solution(mesh):
    placed = (
        P("blocks", "lev", None, None, None),
        P("blocks", None, None, None),
        P("blocks", None, None, None),
        P("blocks", None, None, None),
        P("blocks", "lev", None, None, None),
        P("blocks", None, None),
        P("blocks", None, None),
        P("blocks", None, None),
        P("blocks", None),
        P("blocks"),
        P("blocks", None, None),
    )
    return jax.shard_map(
        functools.partial(local, mesh.shape["blocks"], mesh.shape["lev"]),
        mesh=mesh,
        in_specs=placed,
        out_specs=P("blocks", "lev", None, None, None),
        check_vma=False,
    )
```

profile of v0, /device:TPU:0, one launch (start us, length us, event | category | flops | bytes accessed | tf_op | source)
XLA Modules:
  0.0 13.2 jit_solution(10370638862896980341)
XLA Ops:
  0.7 11.8 %shard_map.100 = f32[8,128,128]{2,1,0:T(8,128)S(1)} custom-call(s32[1,4]{1,0:T(1,128)} %nbr_hbm.1, s32[1,1]{1,0:T(1,128)} %bitcast.10.fold_hbm, s32[4,128]{1,0:T(4,128)} %bitcast.19, f32[8,128,128]{2,1,0:T(8,128)} %bitcast.12, f32[8,128,128]{2,1,0:T(8,128)} %bitcast.13, f32[8,128,128]{2,1,0:T(8,128)} %bitcast.14, f32[8,128,128]{2,1,0:T(8,128)} %bitcast.15, ...), custom_call_target="tpu_custom_call" | custom-call | tf_op jit(solution)/shard_map/pallas_call | solution.py:395
  12.5 0.8 %copy.12 = f32[1,1,8,128,128]{4,3,2,1,0:T(8,128)} copy(f32[1,1,8,128,128]{4,3,2,1,0:T(8,128)S(1)} %bitcast.11) | data formatting | bytes 1048576
where the time goes:
time: 13.4 us; the launch traced here: 13.2 us
  Pallas kernels  11.8 us (88%)
  local copies, waits for them, and re-layouts  0.8 us (6%)
  between operations  0.66 us (5%)
    pallas_call x1, Pallas kernels, local(): pl.pallas_call(functools.partial(kernel, nb, nl), out_shape=pltpu.VMEM(cu...  11.8 us
    unnamed x1, local copies, waits for them, and re-layouts  0.8 us

commit v1 on v0

--- a/solution.py
+++ b/solution.py
@@ -46,12 +46,17 @@
     pay_ref,
     halo_ref,
     part_ref,
+    sum_ref,
+    column_ref,
     parts_ref,
     in_sem,
     edge_send,
     edge_recv,
     part_send,
+    rest_send,
+    column_recv,
     part_recv,
+    ready,
 ):
     t_ref, g_ref = tg_ref.at[0], tg_ref.at[1]
     u_ref, v_ref, w_ref = (flow_ref.at[i] for i in range(3))
@@ -62,22 +67,22 @@
     lev = lax.axis_index("lev")
     late = (block >= nb // 2) & (lev > 0)
 
-    def each_other(visit):
-        def outer(i, carry):
-            there = lax.rem(block + i, nb)
-
-            def inner(j, carry):
-                visit(i * nl + j - 1, {"blocks": there, "lev": lax.rem(lev + j, nl)})
-                return carry
-
-            return lax.fori_loop(0, nl, inner, carry, unroll=unroll)
-
-        def first(j, carry):
-            visit(j - 1, {"blocks": block, "lev": lax.rem(lev + j, nl)})
+    first_column = lev == 0
+
+    def each_block(visit, j, start):
+        def along(i, carry):
+            visit(i, {"blocks": lax.rem(block + i, nb), "lev": j})
             return carry
 
-        lax.fori_loop(1, nb, outer, 0, unroll=unroll)
-        lax.fori_loop(1, nl, first, 0, unroll=unroll)
+        lax.fori_loop(start, nb, along, 0, unroll=unroll)
+
+    def to_rest(visit):
+        for j in range(1, nl):
+            each_block(visit, j, 1)
+
+            @pl.when(lev != j)
+            def _():
+                visit(0, {"blocks": block, "lev": j})
 
     plan = (
         (t_hbm, t_ref, 0),
@@ -99,11 +104,14 @@
 
     barrier = pltpu.get_barrier_semaphore()
 
-    each_other(
-        lambda slot, device: pl.semaphore_signal(
-            barrier, inc=1, device_id=device, device_id_type=MESH
-        )
-    )
+    def signal(i, device):
+        pl.semaphore_signal(barrier, inc=1, device_id=device, device_id_type=MESH)
+
+    @pl.when(first_column)
+    def _():
+        each_block(signal, 0, 1)
+
+    to_rest(signal)
 
     lane = lax.broadcasted_iota(jnp.int32, (rows, cols), 1)
     row = lax.broadcasted_iota(jnp.int32, (rows, cols), 0)
@@ -131,22 +139,48 @@
     )
     part_ref[...] = own_part
 
-    def send_parts():
-        each_other(
-            lambda slot, device: pltpu.make_async_remote_copy(
-                src_ref=part_ref,
-                dst_ref=parts_ref.at[slot],
-                send_sem=part_send,
-                recv_sem=part_recv,
-                device_id=device,
-                device_id_type=MESH,
-            ).start()
-        )
+    sum_ref[...] = own_part
+
+    def send_row(src, dst, send, recv, device):
+        pltpu.make_async_remote_copy(
+            src_ref=src,
+            dst_ref=dst,
+            send_sem=send,
+            recv_sem=recv,
+            device_id=device,
+            device_id_type=MESH,
+        ).start()
+
+    def meet():
+        @pl.when(first_column)
+        def _():
+            pl.semaphore_wait(barrier, nb - 1)
+            each_block(
+                lambda i, device: send_row(
+                    part_ref, column_ref.at[i - 1], part_send, column_recv, device
+                ),
+                0,
+                1,
+            )
+
+        @pl.when(jnp.logical_not(first_column))
+        def _():
+            pl.semaphore_wait(barrier, n - 1)
+            pl.semaphore_signal(
+                ready, inc=1, device_id={"blocks": block, "lev": 0}, device_id_type=MESH
+            )
+
+            def send_part(send):
+                return lambda i, device: send_row(
+                    part_ref, parts_ref.at[(lev - 1) * nb + i], send, part_recv, device
+                )
+
+            each_block(send_part(part_send), 0, 0)
+            to_rest(send_part(rest_send))
 
     @pl.when(late)
     def _():
-        pl.semaphore_wait(barrier, n - 1)
-        send_parts()
+        meet()
 
     def strip(fields):
         wide = jnp.zeros((rows, cols), F32)
@@ -199,7 +233,7 @@
 
     @pl.when(jnp.logical_not(late))
     def _():
-        pl.semaphore_wait(barrier, n - 1)
+        meet()
 
     def send_edges(i, carry):
         pltpu.make_async_remote_copy(
@@ -213,10 +247,6 @@
         return carry
 
     lax.fori_loop(1, nb, send_edges, 0, unroll=unroll)
-
-    @pl.when(jnp.logical_not(late))
-    def _():
-        send_parts()
 
     inverse = 1.0 / shave
     bottom_east = pltpu.roll(bottom, cols - 1, 1)
@@ -300,6 +330,20 @@
     found_t[3] = jnp.where(hit, turned[:levels], found_t[3])
     found_f[3] = jnp.where(hit, -turned[levels:], found_f[3])
 
+    @pl.when(first_column)
+    def _():
+        pltpu.make_async_copy(column_ref, column_ref, column_recv).wait()
+        sum_ref[...] = part_ref[...] + jnp.sum(column_ref[...], axis=0)
+        pl.semaphore_wait(ready, nl - 1)
+        for j in range(1, nl):
+            send_row(
+                sum_ref,
+                parts_ref.at[(j - 1) * nb],
+                rest_send,
+                part_recv,
+                {"blocks": block, "lev": j},
+            )
+
     pltpu.make_async_copy(halo_ref, halo_ref, edge_recv).wait()
 
     def collect(i, carry):
@@ -355,9 +399,7 @@
         x_ref[:, r, :] += gain
 
     pltpu.make_async_copy(parts_ref, parts_ref, part_recv).wait()
-    total = lax.fori_loop(
-        0, n - 1, lambda i, carry: carry + parts_ref[i], part_ref[...], unroll=unroll
-    )
+    total = sum_ref[...] + jnp.sum(parts_ref[...], axis=0)
     total_source = jnp.sum(jnp.where(first_half, total, 0.0), axis=1, keepdims=True)
     total_volume = jnp.sum(jnp.where(first_half, 0.0, total), axis=1, keepdims=True)
     mean = total_source / total_volume
@@ -367,7 +409,19 @@
         out_ref[k] = jnp.where(k < bottom_ref[...], moved - mean, 0.0)
 
     pltpu.make_async_copy(halo_ref, halo_ref, edge_send).wait()
-    pltpu.make_async_copy(parts_ref, parts_ref, part_send).wait()
+
+    def sent(ref, sem):
+        pltpu.make_async_copy(ref, ref, sem).wait()
+
+    @pl.when(first_column)
+    def _():
+        sent(column_ref, part_send)
+        sent(parts_ref.at[: nl - 1], rest_send)
+
+    @pl.when(jnp.logical_not(first_column))
+    def _():
+        sent(parts_ref.at[:nb], part_send)
+        sent(parts_ref.at[: n - nb - 1], rest_send)
 
 
 def local(
@@ -412,12 +466,17 @@
             pltpu.VMEM((nb - 1, 4 * levels, cols), F32),
             pltpu.VMEM((nb - 1, 4 * levels, cols), F32),
             pltpu.VMEM((1, cols), F32),
-            pltpu.VMEM((n - 1, 1, cols), F32),
+            pltpu.VMEM((1, cols), F32),
+            pltpu.VMEM((nb - 1, 1, cols), F32),
+            pltpu.VMEM((n - nb, 1, cols), F32),
             pltpu.SemaphoreType.DMA((7,)),
             pltpu.SemaphoreType.DMA,
             pltpu.SemaphoreType.DMA,
             pltpu.SemaphoreType.DMA,
             pltpu.SemaphoreType.DMA,
+            pltpu.SemaphoreType.DMA,
+            pltpu.SemaphoreType.DMA,
+            pltpu.SemaphoreType.REGULAR,
         ],
         compiler_params=pltpu.CompilerParams(
             collective_id=0, has_side_effects=True, vmem_limit_bytes=grant

time: 13.4 us -> 12.1 us (0.903)
  Pallas kernels: 11.8 us -> 10.5 us
    pallas_call x1, Pallas kernels: 11.8 us -> 10.5 us  [local(): pl.pallas_call(functools.partial(kernel, nb, nl), out_shape=pltpu.VMEM(cu...]
where the time goes in v1:
time: 12.1 us; the launch traced here: 11.9 us
  Pallas kernels  10.5 us (87%)
  local copies, waits for them, and re-layouts  0.8 us (7%)
  between operations  0.66 us (5%)
    pallas_call x1, Pallas kernels, local(): pl.pallas_call(functools.partial(kernel, nb, nl), out_shape=pltpu.VMEM(cu...  10.5 us
    unnamed x1, local copies, waits for them, and re-layouts  0.8 us

profile of v1, /device:TPU:0, one launch (start us, length us, event | category | flops | bytes accessed | tf_op | source)
XLA Modules:
  0.0 11.9 jit_solution(14340959166851691884)
XLA Ops:
  0.7 10.5 %shard_map.100 = f32[8,128,128]{2,1,0:T(8,128)S(1)} custom-call(s32[1,4]{1,0:T(1,128)} %nbr_hbm.1, s32[1,1]{1,0:T(1,128)} %bitcast.10.fold_hbm, s32[4,128]{1,0:T(4,128)} %bitcast.19, f32[8,128,128]{2,1,0:T(8,128)} %bitcast.12, f32[8,128,128]{2,1,0:T(8,128)} %bitcast.13, f32[8,128,128]{2,1,0:T(8,128)} %bitcast.14, f32[8,128,128]{2,1,0:T(8,128)} %bitcast.15, ...), custom_call_target="tpu_custom_call" | custom-call | tf_op jit(solution)/shard_map/pallas_call | solution.py:449
  11.1 0.8 %copy.12 = f32[1,1,8,128,128]{4,3,2,1,0:T(8,128)} copy(f32[1,1,8,128,128]{4,3,2,1,0:T(8,128)S(1)} %bitcast.11) | data formatting | bytes 1048576

commit v2 on v1

--- a/solution.py
+++ b/solution.py
@@ -31,18 +31,19 @@
     g_hbm,
     bottom_hbm,
     shave_hbm,
-    out_ref,
+    x_ref,
+    gain_ref,
+    mean_ref,
+    bottom_ref,
     tg_ref,
     flow_ref,
-    bottom_ref,
     shave_ref,
     nbr_ref,
     fold_ref,
     side_ref,
-    x_ref,
     edge_ref,
+    own_ref,
     pick_ref,
-    gain_ref,
     pay_ref,
     halo_ref,
     part_ref,
@@ -65,7 +66,8 @@
     unroll = n <= 64
     block = lax.axis_index("blocks")
     lev = lax.axis_index("lev")
-    late = (block >= nb // 2) & (lev > 0)
+    far = block >= nb // 2
+    late = far & (lev > 0)
 
     first_column = lev == 0
 
@@ -84,20 +86,29 @@
             def _():
                 visit(0, {"blocks": block, "lev": j})
 
-    plan = (
-        (t_hbm, t_ref, 0),
-        (bottom_hbm, bottom_ref, 1),
-        (shave_hbm, shave_ref, 2),
-        (g_hbm, g_ref, 0),
-        (nbr_hbm, nbr_ref, 3),
-        (fold_hbm, fold_ref, 4),
-        (side_hbm, side_ref, 5),
-        (u_hbm, u_ref, 6),
-        (v_hbm, v_ref, 6),
-        (w_hbm, w_ref, 6),
-    )
-    for src, dst, sem in plan:
+    def load(src, dst, sem):
         pltpu.make_async_copy(src, dst, in_sem.at[sem]).start()
+
+    def load_flow():
+        load(u_hbm, u_ref, 6)
+        load(v_hbm, v_ref, 6)
+
+    load(t_hbm, t_ref, 0)
+
+    @pl.when(first_column)
+    def _():
+        load_flow()
+
+    load(bottom_hbm, bottom_ref, 1)
+    load(shave_hbm, shave_ref, 2)
+    load(g_hbm, g_ref, 7)
+    load(nbr_hbm, nbr_ref, 3)
+    load(fold_hbm, fold_ref, 4)
+    load(side_hbm, side_ref, 5)
+
+    @pl.when(first_column)
+    def _():
+        load(w_hbm, w_ref, 8)
 
     def arrived(ref, sem):
         pltpu.make_async_copy(ref, ref, in_sem.at[sem]).wait()
@@ -117,18 +128,108 @@
     row = lax.broadcasted_iota(jnp.int32, (rows, cols), 0)
     lane_pair = lane // 2
 
+    blank = jnp.zeros((levels, cols), F32)
+
+    def strip(fields):
+        wide = jnp.zeros((rows, cols), F32)
+        for j, field in enumerate(fields):
+            wide = jnp.where(lane_pair == j, pltpu.roll(field(), 2 * j + 1, 1), wide)
+        return wide.T
+
+    def pack_edges():
+        fields = [functools.partial(lambda k: t_ref[k], k) for k in range(levels)]
+        fields += [functools.partial(lambda k: u_ref[k], k) for k in range(levels)]
+        edge_ref[...] = strip(fields)
+        t_north = t_ref[:, rows - 1, :]
+        v_north = v_ref[:, rows - 1, :]
+        t_edges = (
+            edge_ref[pl.ds(1, levels, stride=2), :],
+            edge_ref[pl.ds(0, levels, stride=2), :],
+            t_ref[:, 0, :],
+            t_north,
+        )
+        f_edges = (
+            edge_ref[pl.ds(2 * levels + 1, levels, stride=2), :],
+            edge_ref[pl.ds(2 * levels, levels, stride=2), :],
+            v_ref[:, 0, :],
+            v_north,
+        )
+        mirror = (
+            lax.broadcasted_iota(jnp.int32, (cols, cols), 0)
+            + lax.broadcasted_iota(jnp.int32, (cols, cols), 1)
+            == cols - 1
+        ).astype(F32)
+        turned = jnp.dot(
+            jnp.concatenate([t_north, v_north], 0),
+            mirror,
+            precision=HIGHEST,
+            preferred_element_type=F32,
+        )
+        for s in range(4):
+            own_ref[s] = t_edges[s]
+            own_ref[4 + s] = f_edges[s]
+        own_ref[8] = turned[:levels]
+        own_ref[9] = turned[levels:]
+        arrived(nbr_ref, 3)
+        sides = [nbr_ref[0, s] for s in range(4)]
+
+        def pack(i, carry):
+            there = lax.rem(block + i, nb)
+            t_side, f_side = blank, blank
+            for s in range(4):
+                hit = sides[s] == there
+                t_side = jnp.where(hit, t_edges[s], t_side)
+                f_side = jnp.where(hit, f_edges[s], f_side)
+            pay_ref[i - 1, :levels, :] = t_side
+            pay_ref[i - 1, levels : 2 * levels, :] = f_side
+            pay_ref[i - 1, 2 * levels :, :] = turned
+            return carry
+
+        lax.fori_loop(1, nb, pack, 0, unroll=unroll)
+
+    def send_edges():
+        def send(i, carry):
+            pltpu.make_async_remote_copy(
+                src_ref=pay_ref.at[i - 1],
+                dst_ref=halo_ref.at[i - 1],
+                send_sem=edge_send,
+                recv_sem=edge_recv,
+                device_id={"blocks": lax.rem(block + i, nb), "lev": lev},
+                device_id_type=MESH,
+            ).start()
+            return carry
+
+        lax.fori_loop(1, nb, send, 0, unroll=unroll)
+
+    arrived(t_ref, 0)
+
+    @pl.when(first_column)
+    def _():
+        arrived(flow_ref.at[:2], 6)
+        pack_edges()
+
+    @pl.when(first_column & (block > nb))
+    def _():
+        pl.semaphore_wait(barrier, nb - 1)
+        send_edges()
+
     arrived(bottom_ref, 1)
     arrived(shave_ref, 2)
-    arrived(tg_ref, 0)
+    arrived(g_ref, 7)
+
+    @pl.when(jnp.logical_not(first_column))
+    def _():
+        load_flow()
+        load(w_hbm, w_ref, 8)
+
     bottom = bottom_ref[...]
     shave = shave_ref[...]
     last = bottom - 1
-    source = jnp.zeros((rows, cols), F32)
-    for k in range(levels):
-        thick = jnp.where(k < last, 1.0, jnp.where(k == last, shave, 0.0))
-        source += thick * (RATE * (g_ref[k] - t_ref[k]))
     volume = jnp.where(bottom > 0, last.astype(F32) + shave, 0.0)
-    source = jnp.sum(source, axis=0, keepdims=True)
+    source = jnp.clip(volume, 0.0, 1.0) * (g_ref[0] - t_ref[0])
+    for k in range(1, levels):
+        source += jnp.clip(volume - k, 0.0, 1.0) * (g_ref[k] - t_ref[k])
+    source = RATE * jnp.sum(source, axis=0, keepdims=True)
     volume = jnp.sum(volume, axis=0, keepdims=True)
     half = cols // 2
     first_half = lax.broadcasted_iota(jnp.int32, (1, cols), 1) < half
@@ -154,7 +255,10 @@
     def meet():
         @pl.when(first_column)
         def _():
-            pl.semaphore_wait(barrier, nb - 1)
+            @pl.when(block <= nb)
+            def _():
+                pl.semaphore_wait(barrier, nb - 1)
+
             each_block(
                 lambda i, device: send_row(
                     part_ref, column_ref.at[i - 1], part_send, column_recv, device
@@ -182,71 +286,27 @@
     def _():
         meet()
 
-    def strip(fields):
-        wide = jnp.zeros((rows, cols), F32)
-        for j, field in enumerate(fields):
-            wide = jnp.where(lane_pair == j, pltpu.roll(field(), 2 * j + 1, 1), wide)
-        return wide.T
-
-    arrived(flow_ref, 6)
-    fields = [functools.partial(lambda k: t_ref[k], k) for k in range(levels)]
-    fields += [functools.partial(lambda k: u_ref[k], k) for k in range(levels)]
-    edge_ref[...] = strip(fields)
-    t_east = edge_ref[pl.ds(0, levels, stride=2), :]
-    t_west = edge_ref[pl.ds(1, levels, stride=2), :]
-    u_east = edge_ref[pl.ds(2 * levels, levels, stride=2), :]
-    u_west = edge_ref[pl.ds(2 * levels + 1, levels, stride=2), :]
-    t_south = t_ref[:, 0, :]
-    t_north = t_ref[:, rows - 1, :]
-    v_south = v_ref[:, 0, :]
-    v_north = v_ref[:, rows - 1, :]
-    mirror = (
-        lax.broadcasted_iota(jnp.int32, (cols, cols), 0)
-        + lax.broadcasted_iota(jnp.int32, (cols, cols), 1)
-        == cols - 1
-    ).astype(F32)
-    turned = jnp.dot(
-        jnp.concatenate([t_north, v_north], 0), mirror, precision=HIGHEST, preferred_element_type=F32
-    )
-    t_edges = (t_west, t_east, t_south, t_north)
-    f_edges = (u_west, u_east, v_south, v_north)
-    arrived(nbr_ref, 3)
+    @pl.when(jnp.logical_not(first_column))
+    def _():
+        arrived(flow_ref.at[:2], 6)
+        pack_edges()
+
+    @pl.when(jnp.logical_not(late))
+    def _():
+        meet()
+
+    @pl.when(block <= nb)
+    def _():
+        send_edges()
+
+    arrived(w_ref, 8)
     arrived(fold_ref, 4)
     arrived(side_ref, 5)
+    t_edges = [own_ref[s] for s in range(4)]
+    f_edges = [own_ref[4 + s] for s in range(4)]
+    turned_t, turned_f = own_ref[8], own_ref[9]
     sides = [nbr_ref[0, s] for s in range(4)]
     fold = fold_ref[0, 0]
-    blank = jnp.zeros((levels, cols), F32)
-
-    def pack(i, carry):
-        there = lax.rem(block + i, nb)
-        t_side, f_side = blank, blank
-        for s in range(4):
-            hit = sides[s] == there
-            t_side = jnp.where(hit, t_edges[s], t_side)
-            f_side = jnp.where(hit, f_edges[s], f_side)
-        pay_ref[i - 1, :levels, :] = t_side
-        pay_ref[i - 1, levels : 2 * levels, :] = f_side
-        pay_ref[i - 1, 2 * levels :, :] = turned
-        return carry
-
-    lax.fori_loop(1, nb, pack, 0, unroll=unroll)
-
-    @pl.when(jnp.logical_not(late))
-    def _():
-        meet()
-
-    def send_edges(i, carry):
-        pltpu.make_async_remote_copy(
-            src_ref=pay_ref.at[i - 1],
-            dst_ref=halo_ref.at[i - 1],
-            send_sem=edge_send,
-            recv_sem=edge_recv,
-            device_id={"blocks": lax.rem(block + i, nb), "lev": lev},
-            device_id_type=MESH,
-        ).start()
-        return carry
-
-    lax.fori_loop(1, nb, send_edges, 0, unroll=unroll)
 
     inverse = 1.0 / shave
     bottom_east = pltpu.roll(bottom, cols - 1, 1)
@@ -327,8 +387,8 @@
     found_t = [jnp.where(sides[s] == block, t_edges[s ^ 1], blank) for s in range(4)]
     found_f = [jnp.where(sides[s] == block, f_edges[s ^ 1], blank) for s in range(4)]
     hit = fold == block
-    found_t[3] = jnp.where(hit, turned[:levels], found_t[3])
-    found_f[3] = jnp.where(hit, -turned[levels:], found_f[3])
+    found_t[3] = jnp.where(hit, turned_t, found_t[3])
+    found_f[3] = jnp.where(hit, -turned_f, found_f[3])
 
     @pl.when(first_column)
     def _():
@@ -402,26 +462,32 @@
     total = sum_ref[...] + jnp.sum(parts_ref[...], axis=0)
     total_source = jnp.sum(jnp.where(first_half, total, 0.0), axis=1, keepdims=True)
     total_volume = jnp.sum(jnp.where(first_half, 0.0, total), axis=1, keepdims=True)
-    mean = total_source / total_volume
-
+    mean_ref[...] = jnp.broadcast_to(total_source / total_volume, (1, cols))
+
+    pltpu.make_async_copy(halo_ref, halo_ref, edge_send).wait()
+
+    def sent(ref, sem):
+        pltpu.make_async_copy(ref, ref, sem).wait()
+
+    @pl.when(first_column)
+    def _():
+        sent(column_ref, part_send)
+        sent(parts_ref.at[: nl - 1], rest_send)
+
+    @pl.when(jnp.logical_not(first_column))
+    def _():
+        sent(parts_ref.at[:nb], part_send)
+        sent(parts_ref.at[: n - nb - 1], rest_send)
+
+
+def finish(x_ref, gain_ref, mean_ref, bottom_ref, out_hbm, held_ref, sem):
+    levels, _, cols = x_ref.shape
+    mean = mean_ref[...]
     for k in range(levels):
         moved = x_ref[k] + gain_ref[:, k * cols : (k + 1) * cols]
-        out_ref[k] = jnp.where(k < bottom_ref[...], moved - mean, 0.0)
-
-    pltpu.make_async_copy(halo_ref, halo_ref, edge_send).wait()
-
-    def sent(ref, sem):
-        pltpu.make_async_copy(ref, ref, sem).wait()
-
-    @pl.when(first_column)
-    def _():
-        sent(column_ref, part_send)
-        sent(parts_ref.at[: nl - 1], rest_send)
-
-    @pl.when(jnp.logical_not(first_column))
-    def _():
-        sent(parts_ref.at[:nb], part_send)
-        sent(parts_ref.at[: n - nb - 1], rest_send)
+        held_ref[k] = jnp.where(k < bottom_ref[...], moved - mean, 0.0)
+        pltpu.make_async_copy(held_ref.at[k], out_hbm.at[k], sem).start()
+    pltpu.make_async_copy(held_ref, held_ref, sem).wait()
 
 
 def local(
@@ -446,30 +512,33 @@
     vmem = pl.BlockSpec(memory_space=pltpu.VMEM)
     grant = (14 << 20) + 4 * cols * (8 * levels * nb + 8 * n)
     anywhere = pl.BlockSpec(memory_space=pl.ANY)
-    stepped = pl.pallas_call(
+    kept = pl.pallas_call(
         functools.partial(kernel, nb, nl),
-        out_shape=pltpu.VMEM(cube, F32),
+        out_shape=(
+            pltpu.VMEM(cube, F32),
+            pltpu.VMEM((rows, levels * cols), F32),
+            pltpu.VMEM((1, cols), F32),
+            pltpu.VMEM((rows, cols), jnp.int32),
+        ),
         in_specs=[anywhere] * 10,
-        out_specs=vmem,
+        out_specs=(vmem,) * 4,
         scratch_shapes=[
             pltpu.VMEM((2, *cube), F32),
             pltpu.VMEM((3, *cube), F32),
-            pltpu.VMEM((rows, cols), jnp.int32),
             pltpu.VMEM((rows, cols), F32),
             pltpu.SMEM((1, 4), jnp.int32),
             pltpu.SMEM((1, 1), jnp.int32),
             pltpu.VMEM((4, cols), jnp.int32),
-            pltpu.VMEM(cube, F32),
             pltpu.VMEM((cols, rows), F32),
+            pltpu.VMEM((10, levels, cols), F32),
             pltpu.VMEM((12 * levels, levels * cols), jnp.bfloat16),
-            pltpu.VMEM((rows, levels * cols), F32),
             pltpu.VMEM((nb - 1, 4 * levels, cols), F32),
             pltpu.VMEM((nb - 1, 4 * levels, cols), F32),
             pltpu.VMEM((1, cols), F32),
             pltpu.VMEM((1, cols), F32),
             pltpu.VMEM((nb - 1, 1, cols), F32),
             pltpu.VMEM((n - nb, 1, cols), F32),
-            pltpu.SemaphoreType.DMA((7,)),
+            pltpu.SemaphoreType.DMA((9,)),
             pltpu.SemaphoreType.DMA,
             pltpu.SemaphoreType.DMA,
             pltpu.SemaphoreType.DMA,
@@ -493,6 +562,14 @@
         in_hbm(bottom.reshape(rows, cols)),
         in_hbm(shave_fraction.reshape(rows, cols)),
     )
+    stepped = pl.pallas_call(
+        finish,
+        out_shape=pltpu.HBM(cube, F32),
+        in_specs=[vmem] * 4,
+        out_specs=anywhere,
+        scratch_shapes=[pltpu.VMEM(cube, F32), pltpu.SemaphoreType.DMA],
+        compiler_params=pltpu.CompilerParams(vmem_limit_bytes=2 << 20),
+    )(*kept)
     return stepped.reshape(tracers.shape)
 
 

time: 12.1 us -> 11.8 us (0.975)
  local copies, waits for them, and re-layouts: 0.8 us -> 0 us
  Pallas kernels: 10.5 us -> 11 us
    unnamed x1 -> x0, local copies, waits for them, and re-layouts: 0.8 us -> none
    pallas_call x1 -> x2, Pallas kernels: 10.5 us -> 11 us  [the longest x1 10.2 us: local(): pl.pallas_call(functools.partial(kernel, nb, nl), out_shape=(pltpu.VMEM(c...]
where the time goes in v2:
time: 11.8 us; the launch traced here: 11.6 us
  Pallas kernels  11 us (93%)
  between operations  0.66 us (6%)
    pallas_call x1, Pallas kernels, local(): pl.pallas_call(functools.partial(kernel, nb, nl), out_shape=(pltpu.VMEM(c...  10.2 us
    pallas_call x1, Pallas kernels, local(): pl.pallas_call(finish, out_shape=pltpu.HBM(cube, F32), in_specs=[vmem] *...  0.81 us

profile of v2, /device:TPU:0, one launch (start us, length us, event | category | flops | bytes accessed | tf_op | source)
XLA Modules:
  0.0 11.6 jit_solution(1273943171004344484)
XLA Ops:
  0.7 10.2 %shard_map.100 = (f32[8,128,128]{2,1,0:T(8,128)S(1)}, f32[128,1024]{1,0:T(8,128)S(1)}, f32[1,128]{1,0:T(1,128)S(1)}, s32[128,128]{1,0:T(8,128)S(1)}) custom-call(s32[1,4]{1,0:T(1,128)} %nbr_hbm.1, s32[1,1]{1,0:T(1,128)} %bitcast.10.fold_hbm, s32[4,128]{1,0:T(4,128)} %bitcast.18, f32[8,128,128]{2,1,0:T(8,128)} %bitcast.11, f32[8,128,128]{2,1,0:T(8,128)} %bitcast.12, ...), custom_call_target="tpu_custom_call" | custom-call | tf_op jit(solution)/shard_map/pallas_call | solution.py:515
  10.8 0.8 %shard_map.101 = f32[8,128,128]{2,1,0:T(8,128)} custom-call(f32[8,128,128]{2,1,0:T(8,128)S(1)} %get-tuple-element.9.x_ref, f32[128,1024]{1,0:T(8,128)S(1)} %get-tuple-element.10.gain_ref, f32[1,128]{1,0:T(1,128)S(1)} %get-tuple-element.11.mean_ref, s32[128,128]{1,0:T(8,128)S(1)} %get-tuple-element.12.bottom_ref), custom_call_target="tpu_custom_call" | custom-call | tf_op jit(solution)/shard_map/pallas_call | solution.py:565

commit v3 on v2

--- a/solution.py
+++ b/solution.py
@@ -32,7 +32,6 @@
     bottom_hbm,
     shave_hbm,
     x_ref,
-    gain_ref,
     mean_ref,
     bottom_ref,
     tg_ref,
@@ -67,7 +66,6 @@
     block = lax.axis_index("blocks")
     lev = lax.axis_index("lev")
     far = block >= nb // 2
-    late = far & (lev > 0)
 
     first_column = lev == 0
 
@@ -94,21 +92,16 @@
         load(v_hbm, v_ref, 6)
 
     load(t_hbm, t_ref, 0)
-
-    @pl.when(first_column)
-    def _():
-        load_flow()
-
+    load(g_hbm, g_ref, 0)
     load(bottom_hbm, bottom_ref, 1)
     load(shave_hbm, shave_ref, 2)
-    load(g_hbm, g_ref, 7)
     load(nbr_hbm, nbr_ref, 3)
     load(fold_hbm, fold_ref, 4)
     load(side_hbm, side_ref, 5)
 
     @pl.when(first_column)
     def _():
-        load(w_hbm, w_ref, 8)
+        load_flow()
 
     def arrived(ref, sem):
         pltpu.make_async_copy(ref, ref, in_sem.at[sem]).wait()
@@ -201,26 +194,13 @@
 
         lax.fori_loop(1, nb, send, 0, unroll=unroll)
 
-    arrived(t_ref, 0)
-
-    @pl.when(first_column)
-    def _():
-        arrived(flow_ref.at[:2], 6)
-        pack_edges()
-
-    @pl.when(first_column & (block > nb))
-    def _():
-        pl.semaphore_wait(barrier, nb - 1)
-        send_edges()
-
     arrived(bottom_ref, 1)
     arrived(shave_ref, 2)
-    arrived(g_ref, 7)
+    arrived(tg_ref, 0)
 
     @pl.when(jnp.logical_not(first_column))
     def _():
         load_flow()
-        load(w_hbm, w_ref, 8)
 
     bottom = bottom_ref[...]
     shave = shave_ref[...]
@@ -255,10 +235,7 @@
     def meet():
         @pl.when(first_column)
         def _():
-            @pl.when(block <= nb)
-            def _():
-                pl.semaphore_wait(barrier, nb - 1)
-
+            pl.semaphore_wait(barrier, nb - 1)
             each_block(
                 lambda i, device: send_row(
                     part_ref, column_ref.at[i - 1], part_send, column_recv, device
@@ -282,24 +259,21 @@
             each_block(send_part(part_send), 0, 0)
             to_rest(send_part(rest_send))
 
-    @pl.when(late)
+    @pl.when(far)
     def _():
         meet()
 
-    @pl.when(jnp.logical_not(first_column))
-    def _():
-        arrived(flow_ref.at[:2], 6)
-        pack_edges()
-
-    @pl.when(jnp.logical_not(late))
+    load(w_hbm, w_ref, 7)
+    arrived(flow_ref.at[:2], 6)
+    pack_edges()
+
+    @pl.when(jnp.logical_not(far))
     def _():
         meet()
 
-    @pl.when(block <= nb)
-    def _():
-        send_edges()
-
-    arrived(w_ref, 8)
+    send_edges()
+
+    arrived(w_ref, 7)
     arrived(fold_ref, 4)
     arrived(side_ref, 5)
     t_edges = [own_ref[s] for s in range(4)]
@@ -444,12 +418,14 @@
     rest = wide - high.astype(F32)
     middle = rest.astype(jnp.bfloat16)
     low = (rest - middle.astype(F32)).astype(jnp.bfloat16)
-    gain_ref[...] = lax.dot_general(
+    placed = lax.dot_general(
         jnp.concatenate([high, middle, low], 0),
         pick_ref[...],
         (((0,), (0,)), ((), ())),
         preferred_element_type=F32,
     )
+    for k in range(levels):
+        x_ref[k] += placed[:, k * cols : (k + 1) * cols]
     for s, r in ((2, 0), (3, rows - 1)):
         merged = weight[r : r + 1] * gains[s] + partner_weight[r : r + 1] * pltpu.roll(
             gains[s], cols - 1, 1
@@ -459,7 +435,11 @@
         x_ref[:, r, :] += gain
 
     pltpu.make_async_copy(parts_ref, parts_ref, part_recv).wait()
-    total = sum_ref[...] + jnp.sum(parts_ref[...], axis=0)
+    terms = [sum_ref[...]]
+    terms += [parts_ref[i] for i in range(n - nb)] if unroll else [jnp.sum(parts_ref[...], axis=0)]
+    while len(terms) > 1:
+        terms = [sum(terms[i : i + 2]) for i in range(0, len(terms), 2)]
+    total = terms[0]
     total_source = jnp.sum(jnp.where(first_half, total, 0.0), axis=1, keepdims=True)
     total_volume = jnp.sum(jnp.where(first_half, 0.0, total), axis=1, keepdims=True)
     mean_ref[...] = jnp.broadcast_to(total_source / total_volume, (1, cols))
@@ -480,13 +460,15 @@
         sent(parts_ref.at[: n - nb - 1], rest_send)
 
 
-def finish(x_ref, gain_ref, mean_ref, bottom_ref, out_hbm, held_ref, sem):
+def finish(x_ref, mean_ref, bottom_ref, out_hbm, held_ref, sem):
     levels, _, cols = x_ref.shape
     mean = mean_ref[...]
+    half = x_ref.shape[1] // 2
     for k in range(levels):
-        moved = x_ref[k] + gain_ref[:, k * cols : (k + 1) * cols]
-        held_ref[k] = jnp.where(k < bottom_ref[...], moved - mean, 0.0)
-        pltpu.make_async_copy(held_ref.at[k], out_hbm.at[k], sem).start()
+        for r in (0, half):
+            piece = pl.ds(r, half)
+            held_ref[k, piece] = jnp.where(k < bottom_ref[piece], x_ref[k, piece] - mean, 0.0)
+            pltpu.make_async_copy(held_ref.at[k, piece], out_hbm.at[k, piece], sem).start()
     pltpu.make_async_copy(held_ref, held_ref, sem).wait()
 
 
@@ -516,12 +498,11 @@
         functools.partial(kernel, nb, nl),
         out_shape=(
             pltpu.VMEM(cube, F32),
-            pltpu.VMEM((rows, levels * cols), F32),
             pltpu.VMEM((1, cols), F32),
             pltpu.VMEM((rows, cols), jnp.int32),
         ),
         in_specs=[anywhere] * 10,
-        out_specs=(vmem,) * 4,
+        out_specs=(vmem,) * 3,
         scratch_shapes=[
             pltpu.VMEM((2, *cube), F32),
             pltpu.VMEM((3, *cube), F32),
@@ -538,7 +519,7 @@
             pltpu.VMEM((1, cols), F32),
             pltpu.VMEM((nb - 1, 1, cols), F32),
             pltpu.VMEM((n - nb, 1, cols), F32),
-            pltpu.SemaphoreType.DMA((9,)),
+            pltpu.SemaphoreType.DMA((8,)),
             pltpu.SemaphoreType.DMA,
             pltpu.SemaphoreType.DMA,
             pltpu.SemaphoreType.DMA,
@@ -565,7 +546,7 @@
     stepped = pl.pallas_call(
         finish,
         out_shape=pltpu.HBM(cube, F32),
-        in_specs=[vmem] * 4,
+        in_specs=[vmem] * 3,
         out_specs=anywhere,
         scratch_shapes=[pltpu.VMEM(cube, F32), pltpu.SemaphoreType.DMA],
         compiler_params=pltpu.CompilerParams(vmem_limit_bytes=2 << 20),

time: 11.8 us -> 11.7 us (level)
  no operation moved by 1% of the time
where the time goes in v3:
time: 11.7 us; the launch traced here: 11.5 us
  Pallas kernels  10.9 us (93%)
  between operations  0.66 us (6%)
    pallas_call x1, Pallas kernels, local(): pl.pallas_call(functools.partial(kernel, nb, nl), out_shape=(pltpu.VMEM(c...  10.1 us
    pallas_call x1, Pallas kernels, local(): pl.pallas_call(finish, out_shape=pltpu.HBM(cube, F32), in_specs=[vmem] *...  0.79 us

profile of v3, /device:TPU:0, one launch (start us, length us, event | category | flops | bytes accessed | tf_op | source)
XLA Modules:
  0.0 11.5 jit_solution(17701719078200533828)
XLA Ops:
  0.7 10.1 %shard_map.100 = (f32[8,128,128]{2,1,0:T(8,128)S(1)}, f32[1,128]{1,0:T(1,128)S(1)}, s32[128,128]{1,0:T(8,128)S(1)}) custom-call(s32[1,4]{1,0:T(1,128)} %nbr_hbm.1, s32[1,1]{1,0:T(1,128)} %bitcast.10.fold_hbm, s32[4,128]{1,0:T(4,128)} %bitcast.18, f32[8,128,128]{2,1,0:T(8,128)} %bitcast.11, f32[8,128,128]{2,1,0:T(8,128)} %bitcast.12, ...), custom_call_target="tpu_custom_call" | custom-call | tf_op jit(solution)/shard_map/pallas_call | solution.py:497
  10.8 0.8 %shard_map.101 = f32[8,128,128]{2,1,0:T(8,128)} custom-call(f32[8,128,128]{2,1,0:T(8,128)S(1)} %get-tuple-element.8.x_ref, f32[1,128]{1,0:T(1,128)S(1)} %get-tuple-element.9.mean_ref, s32[128,128]{1,0:T(8,128)S(1)} %get-tuple-element.10.bottom_ref), custom_call_target="tpu_custom_call" | custom-call | tf_op jit(solution)/shard_map/pallas_call | solution.py:546

commit v4 on v3

--- a/solution.py
+++ b/solution.py
@@ -47,13 +47,11 @@
     halo_ref,
     part_ref,
     sum_ref,
-    column_ref,
-    parts_ref,
+    rows_ref,
     in_sem,
     edge_send,
     edge_recv,
     part_send,
-    rest_send,
     column_recv,
     part_recv,
     ready,
@@ -61,11 +59,12 @@
     t_ref, g_ref = tg_ref.at[0], tg_ref.at[1]
     u_ref, v_ref, w_ref = (flow_ref.at[i] for i in range(3))
     levels, rows, cols = t_ref.shape
+    column_ref, parts_ref = rows_ref.at[: nb - 1], rows_ref.at[nb - 1 :]
     n = nb * nl
     unroll = n <= 64
     block = lax.axis_index("blocks")
     lev = lax.axis_index("lev")
-    far = block >= nb // 2
+    far = block >= nb // 4
 
     first_column = lev == 0
 
@@ -90,9 +89,10 @@
     def load_flow():
         load(u_hbm, u_ref, 6)
         load(v_hbm, v_ref, 6)
-
+        load(w_hbm, w_ref, 6)
+
+    load(g_hbm, g_ref, 0)
     load(t_hbm, t_ref, 0)
-    load(g_hbm, g_ref, 0)
     load(bottom_hbm, bottom_ref, 1)
     load(shave_hbm, shave_ref, 2)
     load(nbr_hbm, nbr_ref, 3)
@@ -257,14 +257,13 @@
                 )
 
             each_block(send_part(part_send), 0, 0)
-            to_rest(send_part(rest_send))
+            to_rest(send_part(part_send))
 
     @pl.when(far)
     def _():
         meet()
 
-    load(w_hbm, w_ref, 7)
-    arrived(flow_ref.at[:2], 6)
+    arrived(flow_ref, 6)
     pack_edges()
 
     @pl.when(jnp.logical_not(far))
@@ -273,7 +272,6 @@
 
     send_edges()
 
-    arrived(w_ref, 7)
     arrived(fold_ref, 4)
     arrived(side_ref, 5)
     t_edges = [own_ref[s] for s in range(4)]
@@ -373,7 +371,7 @@
             send_row(
                 sum_ref,
                 parts_ref.at[(j - 1) * nb],
-                rest_send,
+                part_send,
                 part_recv,
                 {"blocks": block, "lev": j},
             )
@@ -451,13 +449,11 @@
 
     @pl.when(first_column)
     def _():
-        sent(column_ref, part_send)
-        sent(parts_ref.at[: nl - 1], rest_send)
+        sent(rows_ref.at[: nb + nl - 2], part_send)
 
     @pl.when(jnp.logical_not(first_column))
     def _():
-        sent(parts_ref.at[:nb], part_send)
-        sent(parts_ref.at[: n - nb - 1], rest_send)
+        sent(rows_ref, part_send)
 
 
 def finish(x_ref, mean_ref, bottom_ref, out_hbm, held_ref, sem):
@@ -517,10 +513,8 @@
             pltpu.VMEM((nb - 1, 4 * levels, cols), F32),
             pltpu.VMEM((1, cols), F32),
             pltpu.VMEM((1, cols), F32),
-            pltpu.VMEM((nb - 1, 1, cols), F32),
-            pltpu.VMEM((n - nb, 1, cols), F32),
-            pltpu.SemaphoreType.DMA((8,)),
-            pltpu.SemaphoreType.DMA,
+            pltpu.VMEM((n - 1, 1, cols), F32),
+            pltpu.SemaphoreType.DMA((7,)),
             pltpu.SemaphoreType.DMA,
             pltpu.SemaphoreType.DMA,
             pltpu.SemaphoreType.DMA,

time: 11.7 us -> 11.7 us (level)
  no operation moved by 1% of the time
where the time goes in v4:
time: 11.7 us; the launch traced here: 11.5 us
  Pallas kernels  10.9 us (93%)
  between operations  0.66 us (6%)
    pallas_call x1, Pallas kernels, local(): pl.pallas_call(functools.partial(kernel, nb, nl), out_shape=(pltpu.VMEM(c...  10.1 us
    pallas_call x1, Pallas kernels, local(): pl.pallas_call(finish, out_shape=pltpu.HBM(cube, F32), in_specs=[vmem] *...  0.79 us

profile of v4, /device:TPU:0, one launch (start us, length us, event | category | flops | bytes accessed | tf_op | source)
XLA Modules:
  0.0 11.5 jit_solution(14353997590916021793)
XLA Ops:
  0.7 10.1 %shard_map.100 = (f32[8,128,128]{2,1,0:T(8,128)S(1)}, f32[1,128]{1,0:T(1,128)S(1)}, s32[128,128]{1,0:T(8,128)S(1)}) custom-call(s32[1,4]{1,0:T(1,128)} %nbr_hbm.1, s32[1,1]{1,0:T(1,128)} %bitcast.10.fold_hbm, s32[4,128]{1,0:T(4,128)} %bitcast.18, f32[8,128,128]{2,1,0:T(8,128)} %bitcast.11, f32[8,128,128]{2,1,0:T(8,128)} %bitcast.12, ...), custom_call_target="tpu_custom_call" | custom-call | tf_op jit(solution)/shard_map/pallas_call | solution.py:493
  10.8 0.8 %shard_map.101 = f32[8,128,128]{2,1,0:T(8,128)} custom-call(f32[8,128,128]{2,1,0:T(8,128)S(1)} %get-tuple-element.8.x_ref, f32[1,128]{1,0:T(1,128)S(1)} %get-tuple-element.9.mean_ref, s32[128,128]{1,0:T(8,128)S(1)} %get-tuple-element.10.bottom_ref), custom_call_target="tpu_custom_call" | custom-call | tf_op jit(solution)/shard_map/pallas_call | solution.py:540
